TPU v7x, 32 devices: a whole 2x2x4 slice. The times are simulated.
32 devices in a mesh: gx: 8 (over y, x, core), gy: 4 (over z).
Axes of the slice: x: 2, y: 2, z: 4, core: 2. Of those that a mesh axis runs over, the one named last changes fastest.
Arguments:
- x_first: bfloat16 [128, 16384], P(None, 'gx'), may hold values from -160 to 160
- x_second: bfloat16 [128, 16384], P(None, 'gx'), may hold values from -160 to 160
- norm_gain: bfloat16 [16384], P('gx'), may hold values from 0.25 to 1.75
- w_qkv: bfloat16 [16384, 18432], P('gx', 'gy'), may hold values from -0.046875 to 0.046875
- w_out: bfloat16 [16384, 16384], P('gy', 'gx'), may hold values from -0.046875 to 0.046875
- cache_keys: bfloat16 [128, 768, 1024], P(('gx', 'gy')), may hold values from -240 to 240
- cache_values: bfloat16 [128, 768, 1024], P(('gx', 'gy')), may hold values from -8 to 8
- lengths: int32 [128], P(('gx', 'gy')), may hold values from 1 to 768, as said below
Outputs:
- out_first: bfloat16 [128, 16384], P('gy', 'gx')
- out_second: bfloat16 [128, 16384], P('gy', 'gx')
Inputs may be any that keep to these rules, and one draw needn't show every extreme that they name: `lengths`: some sequence has exactly 768 filled slots in every draw.
All inputs are finite; a program needn't handle non-finite values.
Results may differ from a plain program's by a relative error of at most 0.012.
The roundings to bfloat16 on the way count: a program that leaves them out, or rounds other values in their place, can miss the bound.
Values may be sent and summed in bfloat16 or wider, within the bound.
A program may use at most 192 MiB of HBM per device.

v0:
```python
import math

import jax
import jax.numpy as jnp
from jax import lax
from jax.sharding import PartitionSpec as P

D = 16384
HEADS = 128
KVH = 8
HD = 128


norm_eps = 1e-05
rotary_base = 500000.0


def rotate_pairs(values, position):
    half_width = values.shape[-1] // 2
    freq = rotary_base ** (-(jnp.arange(half_width, dtype=jnp.float32) * 2.0 / values.shape[-1]))
    angle = position.astype(jnp.float32)[..., None] * freq
    shape = position.shape + (1,) * (values.ndim - position.ndim - 1) + (half_width,)
    cosine = jnp.cos(angle).reshape(shape)
    sine = jnp.sin(angle).reshape(shape)
    first = values[..., :half_width]
    second = values[..., half_width:]
    return jnp.concatenate(
        [first * cosine - second * sine, second * cosine + first * sine], axis=-1
    )


def body(x_first, x_second, norm_gain, w_qkv, w_out, cache_keys, cache_values, lengths):
    rows_dev = lengths.shape[0]
    cache_len = cache_keys.shape[1]
    group_size = HEADS // KVH
    score_scale = 1.0 / math.sqrt(HD)
    keys_heads = jnp.transpose(cache_keys.reshape(rows_dev, cache_len, KVH, HD), (0, 2, 1, 3))
    values_heads = jnp.transpose(cache_values.reshape(rows_dev, cache_len, KVH, HD), (0, 2, 1, 3))
    valid = (jnp.arange(cache_len, dtype=jnp.int32)[None, :] < lengths[:, None])[:, None, None, :]

    def project_local(stacked):
        wide = stacked.astype(jnp.float32)
        squares = jnp.sum(wide * wide, axis=2)
        scaled = (wide * norm_gain.astype(jnp.float32)).astype(jnp.bfloat16)
        block_rows = stacked.shape[1] // lax.axis_size("gx")
        partial_sum = jnp.einsum("sbd,dc->sbc", scaled, w_qkv, preferred_element_type=jnp.float32)
        totals = lax.psum(squares, "gx")
        summed = lax.psum_scatter(partial_sum, "gx", scatter_dimension=1, tiled=True)
        row_squares = lax.dynamic_slice_in_dim(
            totals, lax.axis_index("gx") * block_rows, block_rows, 1
        )
        joined = (summed * lax.rsqrt(row_squares / D + norm_eps)[..., None]).astype(jnp.bfloat16)
        batch_major = lax.all_to_all(joined, "gy", split_axis=1, concat_axis=2, tiled=True)
        batch_major = batch_major.reshape(batch_major.shape[0], rows_dev, KVH, group_size + 2, HD)
        return (
            batch_major[:, :, :, :group_size],
            batch_major[:, :, :, group_size],
            batch_major[:, :, :, group_size + 1],
        )

    def attend(query, new_keys, new_values):
        cache_scores = (
            jnp.einsum("bkgd,bktd->bkgt", query, keys_heads, preferred_element_type=jnp.float32)
            * score_scale
        )
        cache_scores = jnp.where(valid, cache_scores, -jnp.inf)
        extra_scores = (
            jnp.einsum("bkgd,ebkd->bkge", query, new_keys, preferred_element_type=jnp.float32)
            * score_scale
        )
        top = jnp.maximum(jnp.max(cache_scores, axis=-1), jnp.max(extra_scores, axis=-1))[..., None]
        cache_weights = jnp.exp(cache_scores - top)
        extra_weights = jnp.exp(extra_scores - top)
        total = jnp.sum(cache_weights, axis=-1) + jnp.sum(extra_weights, axis=-1)
        mixed = jnp.einsum(
            "bkgt,bktd->bkgd",
            cache_weights.astype(jnp.bfloat16),
            values_heads,
            preferred_element_type=jnp.float32,
        )
        mixed = mixed + jnp.einsum(
            "bkge,ebkd->bkgd",
            extra_weights.astype(jnp.bfloat16),
            new_values,
            preferred_element_type=jnp.float32,
        )
        return (mixed / total[..., None]).astype(jnp.bfloat16).reshape(rows_dev, HEADS * HD)

    def output_local(heads):
        by_heads = lax.all_to_all(heads, "gy", split_axis=2, concat_axis=1, tiled=True)
        partial_out = jnp.einsum(
            "sbh,hd->sbd",
            lax.all_gather(by_heads, "gx", axis=1, tiled=True),
            w_out,
            preferred_element_type=jnp.float32,
        )
        return lax.psum_scatter(partial_out, "gy", scatter_dimension=1, tiled=True).astype(
            jnp.bfloat16
        )

    query_one, key_one, value_one = project_local(x_first[None])
    query_one = rotate_pairs(query_one[0].astype(jnp.float32), lengths).astype(jnp.bfloat16)
    key_one = rotate_pairs(key_one[0].astype(jnp.float32), lengths).astype(jnp.bfloat16)
    value_one = value_one[0]
    heads_one = attend(query_one, key_one[None], value_one[None])
    query_two, key_two, value_two = project_local(x_second[None])
    query_two = rotate_pairs(query_two[0].astype(jnp.float32), lengths + 1).astype(jnp.bfloat16)
    key_two = rotate_pairs(key_two[0].astype(jnp.float32), lengths + 1).astype(jnp.bfloat16)
    value_two = value_two[0]
    heads_two = attend(query_two, jnp.stack([key_one, key_two]), jnp.stack([value_one, value_two]))
    out_first = output_local(heads_one[None])[0]
    out_second = output_local(heads_two[None])[0]
    return (out_first, out_second)


def solution(mesh):
    in_specs = (
        P(None, "gx"),
        P(None, "gx"),
        P("gx"),
        P("gx", "gy"),
        P("gy", "gx"),
        P(("gx", "gy"), None, None),
        P(("gx", "gy"), None, None),
        P(("gx", "gy")),
    )
    out_specs = (P("gy", "gx"), P("gy", "gx"))
    return jax.shard_map(body, mesh=mesh, in_specs=in_specs, out_specs=out_specs, check_vma=False)
```

profile of v0, /device:TPU:0, one launch (start us, length us, event | category | flops | bytes accessed | tf_op | source)
XLA Modules:
  0.0 526.4 jit_solution(171374144711012215)
XLA Ops:
  7.9 10.6 %convolution_bitcast_fusion = f32[1,128,4608]{2,1,0:T(8,128)} fusion(bf16[2048,4608]{1,0:T(8,128)(2,1)} %param.11, bf16[128,2048]{1,0:T(8,128)(2,1)} %param.9, f32[2048]{0:T(1024)S(1)} %convert_element_type.103), kind=kOutput, calls=%fused_computation.6 | convolution fusion | flops 2416705536 | bytes 21766144 | tf_op jit(solution)/shard_map/sbd,dc->sbc/dot_general | solution.py:46
  18.6 10.5 %convolution_bitcast_fusion.1 = f32[1,128,4608]{2,1,0:T(8,128)} fusion(bf16[2048,4608]{1,0:T(8,128)(2,1)} %param.11, bf16[128,2048]{1,0:T(8,128)(2,1)S(1)} %copy-done, f32[2048]{0:T(1024)S(1)} %convert_element_type.103), kind=kOutput, calls=%fused_computation.7 | convolution fusion | flops 2416705536 | bytes 21766144 | tf_op jit(solution)/shard_map/sbd,dc->sbc/dot_general | solution.py:46
  29.5 15.2 %all-reduce = (f32[1,128]{1,0:T(1,128)S(1)}, f32[1,128]{1,0:T(1,128)S(1)}) all-reduce(f32[1,128]{1,0:T(1,128)S(1)} %bitcast.156, f32[1,128]{1,0:T(1,128)S(1)} %bitcast.157), channel_id=1, replica_groups=mesh['gx'=8,'gy'=4] {'gx'}, use_global_device_ids=true, to_apply=%region_2.0 | all-reduce | flops 256 | bytes 2048 | tf_op jit(solution)/shard_map/psum | solution.py:47
  45.0 18.7 %reduce-scatter.9.cloned.1.call-done = f32[1,16,4608]{2,1,0:T(8,128)} async-done(((f32[1,128,4608]{2,1,0:T(8,128)}), f32[1,16,4608]{2,1,0:T(8,128)}) %reduce-scatter.9.cloned.1.call-update) | async-done | bytes 294928 | tf_op jit(solution)/shard_map/reduce_scatter | solution.py:48
  65.6 1.4 reduce.8
  67.7 4.6 all-to-all-start.2
  72.3 37.1 %reduce-scatter.5.cloned.1.call-done = f32[1,16,4608]{2,1,0:T(8,128)} async-done(((f32[1,128,4608]{2,1,0:T(8,128)}), f32[1,16,4608]{2,1,0:T(8,128)}) %reduce-scatter.5.cloned.1.call-update) | async-done | bytes 294928 | tf_op jit(solution)/shard_map/reduce_scatter | solution.py:48
  110.8 1.4 reduce.9
  112.9 4.8 all-to-all-start
  118.9 5.0 all-to-all-done
  125.7 4.9 fusion.58
  133.0 12.9 %copy.79 = bf16[1,4,16384]{1,0,2:T(2,128)(2,1)} copy(bf16[1,4,16384]{2,1,0:T(4,128)(2,1)S(1)} %broadcast_in_dim_reshape.7) | data formatting | bytes 262144 | tf_op jit(solution)/shard_map/broadcast_in_dim;reshape | solution.py:112
  145.9 90.9 %reduce.11 = bf16[16384,4]{1,0:T(8,128)(2,1)} reduce(bf16[16384,1,4]{2,1,0:T(2,128)(2,1)} %bitcast.136, bf16[]{:T(256)} %broadcast.177), dimensions={1}, to_apply=%bitcast.103.reduce_sub_computation | reduce | bytes 262146
  236.8 9.3 %reshape.387 = bf16[4,2,8192]{2,1,0:T(2,128)(2,1)} reshape(bf16[16384,4]{1,0:T(8,128)(2,1)} %reduce.11) | data formatting | bytes 262144
  246.2 3.3 all-to-all-start.3
  249.6 5.8 %all-to-all-done.3 = bf16[4,2,8192]{2,1,0:T(2,128)(2,1)S(1)} async-done(((bf16[4,2,8192]{2,1,0:T(2,128)(2,1)}), bf16[4,2,8192]{2,1,0:T(2,128)(2,1)S(1)}, u32[]{:S(2)}, u32[]{:S(2)}) %all-to-all-start.3) | async-done | bytes 131104 | tf_op jit(solution)/shard_map/all_to_all | solution.py:90
  255.4 11.1 %reshape.388 = bf16[16384,1,4]{2,1,0:T(2,128)(2,1)} reshape(bf16[4,2,8192]{2,1,0:T(2,128)(2,1)S(1)} %all-to-all-done.3) | data formatting | bytes 262144
  266.4 15.5 %copy.80 = bf16[1,4,16384]{2,1,0:T(4,128)(2,1)S(1)} copy(bf16[1,4,16384]{1,0,2:T(2,128)(2,1)} %bitcast.137) | data formatting | bytes 262144 | tf_op jit(solution)/shard_map/all_to_all | solution.py:90
  283.2 4.8 fusion.57
  290.0 13.1 %copy.68 = bf16[1,4,16384]{1,0,2:T(2,128)(2,1)} copy(bf16[1,4,16384]{2,1,0:T(4,128)(2,1)S(1)} %broadcast_in_dim_reshape.6) | data formatting | bytes 262144 | tf_op jit(solution)/shard_map/broadcast_in_dim;reshape | solution.py:111
  303.2 90.7 %reduce.10 = bf16[16384,4]{1,0:T(8,128)(2,1)} reduce(bf16[16384,1,4]{2,1,0:T(2,128)(2,1)} %bitcast.135, bf16[]{:T(256)} %broadcast.177), dimensions={1}, to_apply=%bitcast.99.reduce_sub_computation | reduce | bytes 262146
  393.9 8.7 %reshape.383 = bf16[4,2,8192]{2,1,0:T(2,128)(2,1)S(1)} reshape(bf16[16384,4]{1,0:T(8,128)(2,1)} %reduce.10) | data formatting | bytes 262144
  402.6 8.4 %all_to_all.66 = bf16[4,2,8192]{2,1,0:T(2,128)(2,1)S(1)} all-to-all(bf16[4,2,8192]{2,1,0:T(2,128)(2,1)S(1)} %reshape.383), channel_id=1, replica_groups=mesh['gx'=8,'gy'=4] {'gy'}, dimensions={0} | all-to-all | bytes 262144 | tf_op jit(solution)/shard_map/all_to_all | solution.py:90
  411.0 11.1 %reshape.384 = bf16[16384,1,4]{2,1,0:T(2,128)(2,1)} reshape(bf16[4,2,8192]{2,1,0:T(2,128)(2,1)S(1)} %all_to_all.66) | data formatting | bytes 262144
  422.1 15.4 %copy.69 = bf16[1,4,16384]{2,1,0:T(4,128)(2,1)S(1)} copy(bf16[1,4,16384]{1,0,2:T(2,128)(2,1)} %bitcast.138) | data formatting | bytes 262144 | tf_op jit(solution)/shard_map/all_to_all | solution.py:90
  438.5 9.5 %convolution_bitcast_fusion.2 = f32[1,128,2048]{2,1,0:T(8,128)} fusion(bf16[4096,2048]{1,0:T(8,128)(2,1)} %param.12, bf16[1,128,4096]{2,1,0:T(8,128)(2,1)} %all-gather.5.cloned.1.call-done), kind=kOutput, calls=%fused_computation.12 | convolution fusion | flops 2147483648 | bytes 18874368 | tf_op jit(solution)/shard_map/sbh,hd->sbd/dot_general | solution.py:91
  448.4 11.6 %all-gather.3.cloned.1.call-done = bf16[1,128,4096]{2,1,0:T(8,128)(2,1)} async-done(((bf16[1,16,4096]{2,1,0:T(8,128)(2,1)}), bf16[1,128,4096]{2,1,0:T(8,128)(2,1)}) %all-gather.3.cloned.1.call-update) | async-done | bytes 1048592 | tf_op jit(solution)/shard_map/all_gather | solution.py:93
  460.0 9.4 %convolution_bitcast_fusion.3 = f32[1,128,2048]{2,1,0:T(8,128)} fusion(bf16[4096,2048]{1,0:T(8,128)(2,1)} %param.12, bf16[1,128,4096]{2,1,0:T(8,128)(2,1)} %all-gather.3.cloned.1.call-done), kind=kOutput, calls=%fused_computation.13 | convolution fusion | flops 2147483648 | bytes 18874368 | tf_op jit(solution)/shard_map/sbh,hd->sbd/dot_general | solution.py:91
  469.4 20.0 %reduce-scatter.11.cloned.1.call-done = f32[1,32,2048]{2,1,0:T(8,128)} async-done(((f32[1,128,2048]{2,1,0:T(8,128)}), f32[1,32,2048]{2,1,0:T(8,128)}) %reduce-scatter.11.cloned.1.call-update) | async-done | bytes 262160 | tf_op jit(solution)/shard_map/reduce_scatter | solution.py:97
  489.4 1.6 convert_bitcast_fusion
  491.1 26.4 %reduce-scatter.7.cloned.1.call-done = f32[1,32,2048]{2,1,0:T(8,128)} async-done(((f32[1,128,2048]{2,1,0:T(8,128)}), f32[1,32,2048]{2,1,0:T(8,128)}) %reduce-scatter.7.cloned.1.call-update) | async-done | bytes 262160 | tf_op jit(solution)/shard_map/reduce_scatter | solution.py:97
  517.4 1.6 convert_bitcast_fusion.1
  (87 shorter events, 15.9 us)
Async XLA Ops:
  7.2 56.6 %reduce-scatter.9.cloned.1.call-start = ((), (), s32[]{:S(2)}) async-start(), calls=%async_computation.11 | async-start | bytes 2654208 | tf_op jit(solution)/shard_map/reduce_scatter | solution.py:48
  7.9 10.7 %copy-start = (bf16[128,2048]{1,0:T(8,128)(2,1)S(1)}, bf16[128,2048]{1,0:T(8,128)(2,1)}, u32[]{:S(2)}) copy-start(bf16[128,2048]{1,0:T(8,128)(2,1)} %param.8) | copy-start | bytes 1572868
  18.5 10.8 %copy-start.1 = (bf16[128,2048]{1,0:T(8,128)(2,1)S(1)}, bf16[128,2048]{1,0:T(8,128)(2,1)}, u32[]{:S(2)}) copy-start(bf16[128,2048]{1,0:T(8,128)(2,1)} %param.9) | copy-start | bytes 1572868
  18.6 26.2 %copy-start.2 = (s32[4]{0:T(128)S(1)}, s32[4]{0:T(128)}, u32[]{:S(2)}) copy-start(s32[4]{0:T(128)} %param.15) | copy-start | bytes 52
  18.6 90.9 %reduce-scatter.5.cloned.1.call-start = ((), (), s32[]{:S(2)}) async-start(), calls=%async_computation.8 | async-start | bytes 2654208 | tf_op jit(solution)/shard_map/reduce_scatter | solution.py:48
  67.7 45.2 %all-to-all-start.2 = ((bf16[4,2,9216]{2,1,0:T(2,128)(2,1)}), bf16[4,2,9216]{2,1,0:T(2,128)(2,1)S(1)}, u32[]{:S(2)}, u32[]{:S(2)}) async-start(bf16[4,2,9216]{2,1,0:T(2,128)(2,1)} %reshape.385), calls=%async_computation.5 | async-start | bytes 294912 | tf_op jit(solution)/shard_map/all_to_all | solution.py:53
  112.9 11.0 %all-to-all-start = ((bf16[4,2,9216]{2,1,0:T(2,128)(2,1)}), bf16[4,2,9216]{2,1,0:T(2,128)(2,1)S(1)}, u32[]{:S(2)}, u32[]{:S(2)}) async-start(bf16[4,2,9216]{2,1,0:T(2,128)(2,1)} %reshape.381), calls=%async_computation.1 | async-start | bytes 294912 | tf_op jit(solution)/shard_map/all_to_all | solution.py:53
  125.2 6.3 %slice-start = ((s8[6291456]{0:T(1024)(128)(4,1)}), s8[4194304]{0:T(1024)(128)(4,1)S(1)}, s32[]{:S(2)}) async-start(s8[6291456]{0:T(1024)(128)(4,1)} %bitcast.139), calls=%async_computation.14 | async-start | bytes 8388608
  125.7 5.8 %slice-start.1 = ((s8[6291456]{0:T(1024)(128)(4,1)}), s8[2097152]{0:T(1024)(128)(4,1)S(1)}, s32[]{:S(2)}) async-start(s8[6291456]{0:T(1024)(128)(4,1)} %bitcast.139), calls=%async_computation.15 | async-start | bytes 4194304
  246.2 9.2 %all-to-all-start.3 = ((bf16[4,2,8192]{2,1,0:T(2,128)(2,1)}), bf16[4,2,8192]{2,1,0:T(2,128)(2,1)S(1)}, u32[]{:S(2)}, u32[]{:S(2)}) async-start(bf16[4,2,8192]{2,1,0:T(2,128)(2,1)} %reshape.387), calls=%async_computation.6 | async-start | bytes 262144 | tf_op jit(solution)/shard_map/all_to_all | solution.py:90
  249.5 189.0 %all-gather.5.cloned.1.call-start = ((), (), s32[]{:S(2)}) async-start(), calls=%async_computation.12 | async-start | bytes 1179648 | tf_op jit(solution)/shard_map/all_gather | solution.py:93
  266.4 22.1 %slice-start.2 = ((s8[6291456]{0:T(1024)(128)(4,1)}), s8[2097152]{0:T(1024)(128)(4,1)S(1)}, s32[]{:S(2)}) async-start(s8[6291456]{0:T(1024)(128)(4,1)} %bitcast.141), calls=%async_computation.16 | async-start | bytes 4194304
  282.9 177.1 %all-gather.3.cloned.1.call-start = ((), (), s32[]{:S(2)}) async-start(), calls=%async_computation.9 | async-start | bytes 1179648 | tf_op jit(solution)/shard_map/all_gather | solution.py:93
  283.2 5.3 %slice-start.3 = ((s8[6291456]{0:T(1024)(128)(4,1)}), s8[4194304]{0:T(1024)(128)(4,1)S(1)}, s32[]{:S(2)}) async-start(s8[6291456]{0:T(1024)(128)(4,1)} %bitcast.141), calls=%async_computation.17 | async-start | bytes 8388608
  438.4 51.1 %reduce-scatter.11.cloned.1.call-start = ((), (), s32[]{:S(2)}) async-start(), calls=%async_computation.13 | async-start | bytes 1310720 | tf_op jit(solution)/shard_map/reduce_scatter | solution.py:97
  448.0 69.4 %reduce-scatter.7.cloned.1.call-start = ((), (), s32[]{:S(2)}) async-start(), calls=%async_computation.10 | async-start | bytes 1310720 | tf_op jit(solution)/shard_map/reduce_scatter | solution.py:97
Sparse Core Ops, SparseCore 0:
  18.7 45.0 reduce-scatter.8
  67.1 42.3 reduce-scatter.4
  283.0 21.4 all-gather.4
  438.5 21.4 all-gather.2
  462.1 27.2 reduce-scatter.10
  491.6 25.7 reduce-scatter.6
where the time goes:
time: 534 us; the launch traced here: 526 us
  other arithmetic  193 us (36%)
  waiting for transfers between devices  125 us (23%)
  local copies, waits for them, and re-layouts  104 us (19%)
  matrix products  53.1 us (10%)
  blocking collectives  23.6 us (4%)
  between operations  15 us (3%)
  starting transfers between devices  13.2 us (2%)
    unnamed x6, other arithmetic  184 us
    reduce_scatter x2, waiting for transfers between devices, project_local(): lax.psum_scatter(partial_sum, 'gx', scatter_dimension=1, tiled=True)  55.9 us
    reduce_scatter x2, waiting for transfers between devices, output_local(): lax.psum_scatter(partial_out, 'gy', scatter_dimension=1, tiled=True)  46.4 us
    unnamed x23, local copies, waits for them, and re-layouts  42.4 us
    all_to_all x8, local copies, waits for them, and re-layouts, output_local(): lax.all_to_all(heads, 'gy', split_axis=2, concat_axis=1, tiled=True)  32.7 us
    dot_general x2, matrix products, project_local(): jnp.einsum('sbd,dc->sbc', scaled, w_qkv, preferred_element_type=jnp.float32)  21.1 us
    dot_general x2, matrix products, output_local(): jnp.einsum('sbh,hd->sbd', lax.all_gather(by_heads, 'gx', axis=1, tiled=Tr...  19 us
    psum x1, blocking collectives, project_local(): totals = lax.psum(squares, 'gx')  15.2 us
  transfers between devices with their start and end apart: 9, of which 7 were waited for; matrix products, arithmetic and copies ran while one was open for 35% of the time, Pallas kernels for 0%

commit v1 on v0

v1 whole, which is shorter than its diff:
```python
import functools
import math

import jax
import jax.numpy as jnp
from jax import lax
from jax.experimental import pallas as pl
from jax.experimental.pallas import tpu as pltpu
from jax.sharding import PartitionSpec as P

HD = 128
norm_eps = 1e-05
rotary_base = 500000.0
STEPS = 2
VMEM_LIMIT = 60 * 1024 * 1024


def qkv_kernel(heads_per, x_ref, gain_ref, w_ref, out_ref, scaled_ref):
    step = pl.program_id(0)
    last = pl.num_programs(0) - 1
    outer, inner, _, tile, _ = out_ref.shape

    @pl.when(step == 0)
    def _():
        scaled_ref[...] = (
            x_ref[...].astype(jnp.float32) * gain_ref[...].astype(jnp.float32)
        ).astype(jnp.bfloat16)

    @pl.when(step < last)
    def _():
        product = jnp.dot(scaled_ref[...], w_ref[...], preferred_element_type=jnp.float32)
        for h in range(heads_per):
            out_ref[:, :, h] = product[:, h * HD : (h + 1) * HD].reshape(outer, inner, tile, HD)

    @pl.when(step == last)
    def _():
        wide = x_ref[...].astype(jnp.float32)
        squares = jnp.sum(wide * wide, axis=1, keepdims=True)
        lanes = jnp.broadcast_to(squares, (squares.shape[0], HD)).reshape(outer, inner, tile, HD)
        for h in range(heads_per):
            out_ref[:, :, h] = lanes


def qkv_partial(x, gain, w, outer, inner):
    rows, depth = x.shape
    columns = w.shape[1]
    heads_per = 2
    width = heads_per * HD
    blocks = columns // width
    tile = rows // (outer * inner)
    return pl.pallas_call(
        functools.partial(qkv_kernel, heads_per),
        grid=(blocks + 1,),
        in_specs=[
            pl.BlockSpec((rows, depth), lambda n: (0, 0)),
            pl.BlockSpec((1, depth), lambda n: (0, 0)),
            pl.BlockSpec((depth, width), lambda n: (0, jnp.minimum(n, blocks - 1))),
        ],
        out_specs=pl.BlockSpec(
            (outer, inner, heads_per, tile, HD), lambda n: (0, 0, n, 0, 0)
        ),
        out_shape=jax.ShapeDtypeStruct(
            (outer, inner, columns // HD + heads_per, tile, HD), jnp.float32
        ),
        scratch_shapes=[pltpu.VMEM((rows, depth), jnp.bfloat16)],
        compiler_params=pltpu.CompilerParams(vmem_limit_bytes=VMEM_LIMIT),
    )(x, gain, w)


def attend_kernel(
    groups, size, rows, lengths_ref, x_ref, cos_ref, sin_ref, keys_ref, values_ref, out_ref,
    in_ref, mix_ref,
):
    row = pl.program_id(0)
    tile = STEPS * rows
    per = size + 2
    slots = keys_ref.shape[1]
    scale = 1.0 / math.sqrt(HD)

    @pl.when(row == 0)
    def _():
        for k in range(groups):
            base = k * per
            turn = x_ref[base : base + size + 1].astype(jnp.float32)
            turned = turn * cos_ref[...][None] + pltpu.roll(turn, HD // 2, 2) * sin_ref[...][None]
            turned = turned.astype(jnp.bfloat16).astype(jnp.float32)
            in_ref[base * tile : (base + size + 1) * tile] = turned.reshape((size + 1) * tile, HD)
            in_ref[(base + size + 1) * tile : (base + per) * tile] = x_ref[base + size + 1].astype(
                jnp.float32
            )

    length = lengths_ref[row]
    valid = lax.broadcasted_iota(jnp.int32, (1, slots), 1) < length
    late = lax.broadcasted_iota(jnp.int32, (STEPS * size, 1), 0) >= size
    for k in range(groups):
        base = k * per * tile
        query = jnp.concatenate(
            [
                in_ref[pl.ds(base + s * rows + row, size, stride=tile), :]
                for s in range(STEPS)
            ],
            axis=0,
        )
        new_keys = [in_ref[pl.ds(base + size * tile + s * rows + row, 1), :] for s in range(STEPS)]
        new_values = [
            in_ref[pl.ds(base + (size + 1) * tile + s * rows + row, 1), :] for s in range(STEPS)
        ]
        columns = slice(k * HD, (k + 1) * HD)
        scores = (
            lax.dot_general(
                query.astype(jnp.bfloat16),
                keys_ref[0, :, columns],
                (((1,), (1,)), ((), ())),
                preferred_element_type=jnp.float32,
            )
            * scale
        )
        scores = jnp.where(valid, scores, -jnp.inf)
        extra_one = jnp.sum(query * new_keys[0], axis=1, keepdims=True) * scale
        extra_two = jnp.sum(query * new_keys[1], axis=1, keepdims=True) * scale
        extra_two = jnp.where(late, extra_two, -jnp.inf)
        top = jnp.maximum(
            jnp.max(scores, axis=1, keepdims=True), jnp.maximum(extra_one, extra_two)
        )
        weights = jnp.exp(scores - top)
        weight_one = jnp.exp(extra_one - top)
        weight_two = jnp.exp(extra_two - top)
        total = jnp.sum(weights, axis=1, keepdims=True) + weight_one + weight_two
        mixed = jnp.dot(
            weights.astype(jnp.bfloat16),
            values_ref[0, :, columns],
            preferred_element_type=jnp.float32,
        )
        mixed = (
            mixed
            + weight_one.astype(jnp.bfloat16).astype(jnp.float32) * new_values[0]
            + weight_two.astype(jnp.bfloat16).astype(jnp.float32) * new_values[1]
        )
        mixed = mixed / total
        for s in range(STEPS):
            mix_ref[pl.ds(k * size * tile + s * rows + row, size, stride=tile), :] = mixed[
                s * size : (s + 1) * size
            ]

    @pl.when(row == rows - 1)
    def _():
        out_ref[...] = mix_ref[...].reshape(out_ref.shape).astype(jnp.bfloat16)


def attend(joined, cosine, sine, keys, values, lengths):
    rows, slots, width = keys.shape
    groups = width // HD
    heads, tile, _ = joined.shape
    size = heads // groups - 2
    whole = lambda r, lens: (0, 0)
    return pl.pallas_call(
        functools.partial(attend_kernel, groups, size, rows),
        grid_spec=pltpu.PrefetchScalarGridSpec(
            num_scalar_prefetch=1,
            grid=(rows,),
            in_specs=[
                pl.BlockSpec((heads, tile, HD), lambda r, lens: (0, 0, 0)),
                pl.BlockSpec((tile, HD), whole),
                pl.BlockSpec((tile, HD), whole),
                pl.BlockSpec((1, slots, width), lambda r, lens: (r, 0, 0)),
                pl.BlockSpec((1, slots, width), lambda r, lens: (r, 0, 0)),
            ],
            out_specs=pl.BlockSpec((groups * size, tile, HD), lambda r, lens: (0, 0, 0)),
            scratch_shapes=[
                pltpu.VMEM((heads * tile, HD), jnp.float32),
                pltpu.VMEM((groups * size * tile, HD), jnp.float32),
            ],
        ),
        out_shape=jax.ShapeDtypeStruct((groups * size, tile, HD), jnp.bfloat16),
        compiler_params=pltpu.CompilerParams(vmem_limit_bytes=VMEM_LIMIT),
    )(lengths, joined, cosine, sine, keys, values)


def out_kernel(x_ref, w_ref, out_ref, flat_ref):
    @pl.when(pl.program_id(0) == 0)
    def _():
        for h in range(x_ref.shape[2]):
            flat_ref[:, h * HD : (h + 1) * HD] = (
                x_ref[:, :, h].astype(jnp.float32).reshape(flat_ref.shape[0], HD)
            ).astype(jnp.bfloat16)

    out_ref[...] = jnp.dot(flat_ref[...], w_ref[...], preferred_element_type=jnp.float32)


def out_partial(heads, w):
    outer, inner, count, tile, _ = heads.shape
    rows = outer * inner * tile
    depth, columns = w.shape
    width = min(256, columns)
    return pl.pallas_call(
        out_kernel,
        grid=(columns // width,),
        in_specs=[
            pl.BlockSpec(heads.shape, lambda n: (0, 0, 0, 0, 0)),
            pl.BlockSpec((depth, width), lambda n: (0, n)),
        ],
        out_specs=pl.BlockSpec((rows, width), lambda n: (0, n)),
        out_shape=jax.ShapeDtypeStruct((rows, columns), jnp.float32),
        scratch_shapes=[pltpu.VMEM((rows, depth), jnp.bfloat16)],
        compiler_params=pltpu.CompilerParams(vmem_limit_bytes=VMEM_LIMIT),
    )(heads, w)


def body(x_first, x_second, norm_gain, w_qkv, w_out, cache_keys, cache_values, lengths):
    outer, inner = lax.axis_size("gx"), lax.axis_size("gy")
    rows = lengths.shape[0]
    tile = STEPS * rows
    depth = x_first.shape[1]
    width = depth * outer
    heads_here = w_qkv.shape[1] // HD

    stacked = jnp.stack(
        [x.reshape(outer * inner, rows, depth) for x in (x_first, x_second)], axis=1
    ).reshape(outer * inner * tile, depth)
    half = HD // 2
    freq = rotary_base ** (-(jnp.arange(half, dtype=jnp.float32) * 2.0 / HD))
    position = jnp.concatenate([lengths + s for s in range(STEPS)])
    angle = position.astype(jnp.float32)[:, None] * freq
    cosine = jnp.tile(jnp.cos(angle), (1, 2))
    sine = jnp.concatenate([-jnp.sin(angle), jnp.sin(angle)], axis=1)

    partial_sum = qkv_partial(stacked, norm_gain[None], w_qkv, outer, inner)
    summed = lax.psum_scatter(partial_sum, "gx", scatter_dimension=0, tiled=True)[0]
    squares = summed[:, heads_here : heads_here + 1]
    joined = (summed[:, :heads_here] * lax.rsqrt(squares / width + norm_eps)).astype(jnp.bfloat16)
    joined = lax.all_to_all(joined, "gy", split_axis=0, concat_axis=0, tiled=True)
    joined = joined.reshape(inner * heads_here, tile, HD)

    heads = attend(joined, cosine, sine, cache_keys, cache_values, lengths)
    heads = heads.reshape(inner, heads.shape[0] // inner, tile, HD)
    heads = lax.all_to_all(heads, "gy", split_axis=0, concat_axis=0, tiled=True)
    heads = lax.all_gather(heads, "gx", axis=0, tiled=False)
    partial_out = out_partial(heads, w_out)
    done = lax.psum_scatter(partial_out, "gy", scatter_dimension=0, tiled=True)
    done = done.astype(jnp.bfloat16).reshape(-1, STEPS, rows, partial_out.shape[1])
    return tuple(done[:, s].reshape(-1, partial_out.shape[1]) for s in range(STEPS))


def solution(mesh):
    in_specs = (
        P(None, "gx"),
        P(None, "gx"),
        P("gx"),
        P("gx", "gy"),
        P("gy", "gx"),
        P(("gx", "gy"), None, None),
        P(("gx", "gy"), None, None),
        P(("gx", "gy")),
    )
    out_specs = (P("gy", "gx"), P("gy", "gx"))
    return jax.shard_map(body, mesh=mesh, in_specs=in_specs, out_specs=out_specs, check_vma=False)
```

time: 534 us -> 224 us (0.42); the launches traced: 526 us -> 223 us
  other arithmetic: 193 us -> 5.18 us
  local copies, waits for them, and re-layouts: 104 us -> 7.2 us
  matrix products: 53.1 us -> 0 us
  Pallas kernels: 0 us -> 45.2 us
  blocking collectives: 23.6 us -> 11.3 us
  waiting for transfers between devices: 125 us -> 136 us
  starting transfers between devices: 13.2 us -> 4.67 us
    unnamed x6 -> x0, other arithmetic: 184 us -> none
    dot_general x11 -> x0, matrix products: 53.1 us -> none  [the longest x2 21.1 us: project_local(): jnp.einsum('sbd,dc->sbc', scaled, w_qkv, preferred_element_type=jnp.float32)]
    pallas_call x0 -> x3, Pallas kernels: none -> 45.2 us  [the longest x1 18.7 us: qkv_partial(): pl.pallas_call(functools.partial(qkv_kernel, heads_per), grid=(blocks + 1...]
    unnamed x23 -> x6, local copies, waits for them, and re-layouts: 42.4 us -> 0.72 us
    all_to_all x14 -> x0, local copies, waits for them, and re-layouts: 34.6 us -> none  [the longest x8 32.7 us: output_local(): lax.all_to_all(heads, 'gy', split_axis=2, concat_axis=1, tiled=True)]
    another operation x4 -> x6, local copies, waits for them, and re-layouts: 26.1 us -> 4.53 us  [the longest x2 2.48 us: body(): jnp.stack([x.reshape(outer * inner, rows, depth) for x in (x_first, x_sec...]
    psum x1 -> x0, blocking collectives: 15.2 us -> none  [project_local(): totals = lax.psum(squares, 'gx')]
    all_gather x2 -> x1, waiting for transfers between devices: 11.6 us -> 26.2 us  [body(): heads = lax.all_gather(heads, 'gx', axis=0, tiled=False)]
  transfers between devices with their start and end apart: 9 -> 4, of which waited for: 7 -> 4; matrix products, arithmetic and copies ran while one was open for 35% -> 1% of each run, Pallas kernels for 0% -> 0%
where the time goes in v1:
time: 224 us; the launch traced here: 223 us
  waiting for transfers between devices  136 us (61%)
  Pallas kernels  45.2 us (20%)
  between operations  13.8 us (6%)
  blocking collectives  11.3 us (5%)
  local copies, waits for them, and re-layouts  7.2 us (3%)
  other arithmetic  5.18 us (2%)
  starting transfers between devices  4.67 us (2%)
    reduce_scatter x1, waiting for transfers between devices, body(): lax.psum_scatter(partial_sum, 'gx', scatter_dimension=0, tiled=True)[0]  57.9 us
    reduce_scatter x1, waiting for transfers between devices, body(): done = lax.psum_scatter(partial_out, 'gy', scatter_dimension=0, tiled=True)  43.8 us
    all_gather x1, waiting for transfers between devices, body(): heads = lax.all_gather(heads, 'gx', axis=0, tiled=False)  26.2 us
    pallas_call x1, Pallas kernels, qkv_partial(): pl.pallas_call(functools.partial(qkv_kernel, heads_per), grid=(blocks + 1...  18.7 us
    pallas_call x1, Pallas kernels, attend(): pl.pallas_call(functools.partial(attend_kernel, groups, size, rows), grid...  13.8 us
    pallas_call x1, Pallas kernels, out_partial(): pl.pallas_call(out_kernel, grid=(columns // width,), in_specs=[pl.BlockSp...  12.7 us
    all_to_all x1, blocking collectives, body(): heads = lax.all_to_all(heads, 'gy', split_axis=0, concat_axis=0, tiled=True)  11.3 us
    all_to_all x1, waiting for transfers between devices, body(): lax.all_to_all(joined, 'gy', split_axis=0, concat_axis=0, tiled=True)  7.91 us
  transfers between devices with their start and end apart: 4, of which 4 were waited for; matrix products, arithmetic and copies ran while one was open for 1% of the time, Pallas kernels for 0%

profile of v1, /device:TPU:0, one launch (start us, length us, event | category | flops | bytes accessed | tf_op | source)
XLA Modules:
  0.0 223.2 jit_solution(13736544586612227737)
XLA Ops:
  7.2 0.0 reduce-scatter.3.cloned.1.call-start
  7.2 1.2 stack_reshape.7
  8.5 1.2 stack_reshape.6
  9.7 0.7 pad_maximum_fusion
  10.4 1.1 reshape.67.x_ref
  11.5 0.6 broadcast_in_dim.2.gain_ref
  12.1 18.7 %shard_map.95 = f32[8,4,38,8,128]{4,3,2,1,0:T(8,128)} custom-call(bf16[256,2048]{1,0:T(8,128)(2,1)} %reshape.67.x_ref, bf16[1,2048]{1,0:T(2,128)(2,1)} %broadcast_in_dim.2.gain_ref, bf16[2048,4608]{1,0:T(8,128)(2,1)} %w_ref.2), custom_call_target="tpu_custom_call" | custom-call | tf_op jit(solution)/shard_map/pallas_call | solution.py:51
  30.9 0.0 reduce-scatter.3.cloned.1.call-update
  30.9 0.0 copy-done.2
  30.9 57.9 %reduce-scatter.3.cloned.1.call-done = f32[1,4,38,8,128]{4,3,2,1,0:T(8,128)} async-done(((f32[8,4,38,8,128]{4,3,2,1,0:T(8,128)}), f32[1,4,38,8,128]{4,3,2,1,0:T(8,128)}) %reduce-scatter.3.cloned.1.call-update) | async-done | bytes 622608 | tf_op jit(solution)/shard_map/reduce_scatter | solution.py:228
  88.8 0.7 fusion.3
  89.6 1.8 fusion
  91.4 4.6 %all-to-all-start = ((bf16[4,36,8,128]{3,2,1,0:T(8,128)(2,1)}), bf16[4,36,8,128]{3,2,1,0:T(8,128)(2,1)S(1)}, u32[]{:S(2)}, u32[]{:S(2)}) async-start(bf16[4,36,8,128]{3,2,1,0:T(8,128)(2,1)} %fusion), calls=%async_computation.1 | async-start | bytes 589824 | tf_op jit(solution)/shard_map/all_to_all | solution.py:231
  96.0 0.1 add_convert_fusion
  96.1 0.1 fusion.4
  96.2 0.7 tile.10.cos_ref
  96.9 0.7 pad_maximum_fusion.1.sin_ref
  97.5 7.9 %all-to-all-done = bf16[4,36,8,128]{3,2,1,0:T(8,128)(2,1)S(1)} async-done(((bf16[4,36,8,128]{3,2,1,0:T(8,128)(2,1)}), bf16[4,36,8,128]{3,2,1,0:T(8,128)(2,1)S(1)}, u32[]{:S(2)}, u32[]{:S(2)}) %all-to-all-start) | async-done | bytes 294944 | tf_op jit(solution)/shard_map/all_to_all | solution.py:231
  105.4 0.7 copy-done
  106.1 13.8 %shard_map.96 = bf16[128,8,128]{2,1,0:T(8,128)(2,1)} custom-call(s32[4]{0:T(128)} %lengths_ref.1, bf16[144,8,128]{2,1,0:T(8,128)(2,1)} %bitcast.11, f32[8,128]{1,0:T(8,128)} %tile.10.cos_ref, f32[8,128]{1,0:T(8,128)} %pad_maximum_fusion.1.sin_ref, bf16[4,768,1024]{2,1,0:T(8,128)(2,1)} %keys_ref.1, bf16[4,768,1024]{2,1,0:T(8,128)(2,1)} %values_ref.1), custom_call_target="tpu_custom_call" | custom-call | tf_op jit(solution)/shard_map/pallas_call | solution.py:156
  120.0 11.3 %all_to_all.10 = bf16[4,32,8,128]{3,2,1,0:T(8,128)(2,1)} all-to-all(bf16[4,32,8,128]{3,2,1,0:T(8,128)(2,1)} %bitcast.12), channel_id=1, replica_groups=mesh['gx'=8,'gy'=4] {'gy'}, dimensions={0} | all-to-all | bytes 524288 | tf_op jit(solution)/shard_map/all_to_all | solution.py:236
  131.3 0.0 all-gather.3.cloned.1.call-update
  131.3 0.0 reduce-scatter.5.cloned.1.call-start
  131.4 26.2 %all-gather.3.cloned.1.call-done = bf16[32,32,8,128]{3,2,1,0:T(8,128)(2,1)} async-done(((bf16[4,32,8,128]{3,2,1,0:T(8,128)(2,1)}), bf16[32,32,8,128]{3,2,1,0:T(8,128)(2,1)}) %all-gather.3.cloned.1.call-update) | async-done | bytes 2097168 | tf_op jit(solution)/shard_map/all_gather | solution.py:237
  157.5 12.7 %shard_map.97 = f32[256,2048]{1,0:T(8,128)} custom-call(bf16[8,4,32,8,128]{4,3,2,1,0:T(8,128)(2,1)} %bitcast.8, bf16[4096,2048]{1,0:T(8,128)(2,1)} %w_ref.3), custom_call_target="tpu_custom_call" | custom-call | tf_op jit(solution)/shard_map/pallas_call | solution.py:195
  170.2 0.0 reduce-scatter.5.cloned.1.call-update
  170.2 43.8 %reduce-scatter.5.cloned.1.call-done = f32[64,2048]{1,0:T(8,128)} async-done(((f32[256,2048]{1,0:T(8,128)}), f32[64,2048]{1,0:T(8,128)}) %reduce-scatter.5.cloned.1.call-update) | async-done | bytes 524304 | tf_op jit(solution)/shard_map/reduce_scatter | solution.py:239
  214.0 1.1 convert_element_type.15
  215.1 0.1 reshape.70
  215.2 0.1 fusion.5
  215.3 0.7 reshape_squeeze.6
  216.0 0.7 reshape_squeeze.7
  (8 shorter events, 0.0 us)
Async XLA Ops:
  7.2 4.4 %copy-start.1 = (bf16[2048]{0:T(1024)(128)(2,1)S(1)}, bf16[2048]{0:T(1024)(128)(2,1)}, u32[]{:S(2)}) copy-start(bf16[2048]{0:T(1024)(128)(2,1)} %param.10) | copy-start | bytes 12292
  7.2 81.7 %reduce-scatter.3.cloned.1.call-start = ((), (), s32[]{:S(2)}) async-start(), calls=%async_computation.4 | async-start | bytes 5603328 | tf_op jit(solution)/shard_map/reduce_scatter | solution.py:228
  12.1 18.8 %copy-start.2 = (s32[4]{0:T(128)S(1)}, s32[4]{0:T(128)}, u32[]{:S(2)}) copy-start(s32[4]{0:T(128)} %lengths_ref.1) | copy-start | bytes 52
  91.4 14.0 %all-to-all-start = ((bf16[4,36,8,128]{3,2,1,0:T(8,128)(2,1)}), bf16[4,36,8,128]{3,2,1,0:T(8,128)(2,1)S(1)}, u32[]{:S(2)}, u32[]{:S(2)}) async-start(bf16[4,36,8,128]{3,2,1,0:T(8,128)(2,1)} %fusion), calls=%async_computation.1 | async-start | bytes 589824 | tf_op jit(solution)/shard_map/all_to_all | solution.py:231
  96.0 61.5 %all-gather.3.cloned.1.call-start = ((), (), s32[]{:S(2)}) async-start(), calls=%async_computation.6 | async-start | bytes 2359296 | tf_op jit(solution)/shard_map/all_gather | solution.py:237
  105.4 0.7 copy-start
  131.3 82.7 %reduce-scatter.5.cloned.1.call-start = ((), (), s32[]{:S(2)}) async-start(), calls=%async_computation.5 | async-start | bytes 2621440 | tf_op jit(solution)/shard_map/reduce_scatter | solution.py:239
Sparse Core Ops, SparseCore 0:
  31.0 57.7 reduce-scatter.2
  131.4 26.0 all-gather.2
  170.3 43.6 reduce-scatter.4
